TPU v7x, 512 devices: a whole 4x4x16 slice. The times are simulated.
512 devices in a mesh: sub: 64 (over z, y), harm: 8 (over x, core).
Axes of the slice: x: 4, y: 4, z: 16, core: 2. Of those that a mesh axis runs over, the one named last changes fastest.
Arguments:
- flex: float32 [64, 8, 768, 768], P('sub', 'harm'), may hold values from -1 to 4, as said below
- loads: float32 [64, 8, 768, 256], P('sub', 'harm'), may hold values from -4 to 4
- side: int32 [64, 12], P('sub'), may hold values from -1 to 1, as said below
- partner: int32 [64, 12], P('sub'), may hold values from 0 to 11, as said below
- contact_blocks: int32 [64, 4], P('sub'), may hold values from 0 to 11, all different within a row
- contact_stiff: float32 [64, 256], P('sub'), may hold values from 0.01 to 0.1
Outputs:
- multipliers: float32 [64, 8, 768, 256], P('sub', 'harm')
- contact_force: float32 [64, 8, 256, 256], P('sub', 'harm')
Inputs may be any that keep to these rules, and one draw needn't show every extreme that they name: Block b of subdomain s is shared with subdomain s + 1 (cyclic) where side is 1, with s - 1 where it is -1, with none where it is 0. Each subdomain shares 1 to 4 blocks with each neighbour, and the pairing through partner is mutual. `partner`: A block with side 0 names itself. `flex`: symmetric positive definite.
All inputs are finite; a program needn't handle non-finite values.
Results may differ from a plain program's by a relative error of at most 0.0003.
Values sent between devices are 32-bit elements; how exact they have to be, the bound alone decides.
A program may use at most 64 MiB of HBM per device.

v0:
```python
import math

import jax
import jax.numpy as jnp
from jax import lax
from jax.sharding import PartitionSpec as P

TIMES = 64
ROUNDS = 2
UPDATES = 2


precise = lax.Precision.HIGHEST
tiny_value = 1e-06


def extended(cells, sides, width):
    for axis, dim in sides:
        count = lax.axis_size(axis)
        head = lax.slice_in_dim(cells, 0, width, axis=dim)
        tail = lax.slice_in_dim(cells, cells.shape[dim] - width, cells.shape[dim], axis=dim)
        cells = jnp.concatenate(
            [
                lax.ppermute(tail, axis, [(i, (i + 1) % count) for i in range(count)]),
                cells,
                lax.ppermute(head, axis, [((i + 1) % count, i) for i in range(count)]),
            ],
            axis=dim,
        )
    return cells


def wave_tables(harm_count):
    time_points = jnp.arange(TIMES, dtype=jnp.float32)
    harm_orders = jnp.arange(1, harm_count + 1, dtype=jnp.float32)
    phases = 2.0 * math.pi / TIMES * time_points[:, None] * harm_orders[None, :]
    return (jnp.cos(phases), jnp.sin(phases))


def apply_flex(flex, field):
    return jnp.einsum("hij,hjc->hic", flex, field, precision=precise)


def opposite_whole(trace, side, partner):
    local_harms, iface_rows, columns = trace.shape
    block_count = side.shape[0]
    stacked = trace.reshape(1, local_harms, block_count, iface_rows // block_count, columns)
    padded = extended(stacked, (("sub", 0),), 1)
    picked = jax.vmap(lambda one: one[side + 1, partner], in_axes=1)(padded)
    return picked.reshape(trace.shape)


def to_coefficients(cubic_term, cos_table, sin_table):
    cos_coef = 2.0 / TIMES * jnp.einsum("tk,tnr->krn", cos_table, cubic_term, precision=precise)
    sin_coef = 2.0 / TIMES * jnp.einsum("tk,tnr->krn", sin_table, cubic_term, precision=precise)
    stacked = jnp.stack([cos_coef, sin_coef], axis=-1)
    return stacked.reshape(stacked.shape[0], stacked.shape[1], stacked.shape[2] * 2)


def time_signal(piece, cos_table, sin_table):
    harmonics, row_count, col_width = piece.shape
    shaped = piece.reshape(harmonics, row_count, col_width // 2, 2)
    signal = jnp.einsum("tk,krn->tnr", cos_table, shaped[..., 0], precision=precise)
    return signal + jnp.einsum("tk,krn->tnr", sin_table, shaped[..., 1], precision=precise)


def contact_cycle(contact_coef):
    piece = lax.all_to_all(contact_coef, "harm", split_axis=2, concat_axis=0, tiled=True)
    cos_table, sin_table = wave_tables(piece.shape[0])
    signal = time_signal(piece, cos_table, sin_table)
    coeffs = to_coefficients(signal * signal * signal, cos_table, sin_table)
    return lax.all_to_all(coeffs, "harm", split_axis=0, concat_axis=2, tiled=True)


def per_device(flex, loads, side, partner, contact_blocks, contact_stiff):
    flex = flex[0]
    loads = loads[0]
    side = side[0]
    partner = partner[0]
    contact_blocks = contact_blocks[0]
    contact_stiff = contact_stiff[0]
    local_harms, iface_rows, columns = loads.shape
    block_count = side.shape[0]
    block_rows = iface_rows // block_count
    block_shape = (local_harms, block_count, block_rows, columns)
    multipliers = jnp.zeros_like(loads)
    trace = loads
    contact_force = None
    for outer in range(ROUNDS):
        if outer > 0:
            trace = apply_flex(flex, multipliers) + loads
        for inner in range(UPDATES):
            neighbours = opposite_whole(trace, side, partner)
            jump = trace - neighbours
            flex_image = apply_flex(flex, jump)
            squares, curvature = lax.psum(
                (jnp.sum(jump * jump, axis=1), jnp.sum(jump * flex_image, axis=1)), "sub"
            )
            step_size = (squares / (curvature + tiny_value))[:, None, :]
            multipliers = multipliers - step_size * jump
            trace = trace - step_size * flex_image
        contact_coef = trace.reshape(block_shape)[:, contact_blocks].reshape(
            local_harms, -1, columns
        )
        contact_force = contact_cycle(contact_coef) * contact_stiff[None, :, None]
        returned = contact_force.reshape(local_harms, contact_blocks.shape[0], block_rows, columns)
        multipliers = (
            multipliers.reshape(block_shape)
            .at[:, contact_blocks]
            .add(-returned)
            .reshape(loads.shape)
        )
    return (multipliers[None], contact_force[None])


def solution(mesh):
    return jax.shard_map(
        per_device,
        mesh=mesh,
        in_specs=(
            P("sub", "harm", None, None),
            P("sub", "harm", None, None),
            P("sub", None),
            P("sub", None),
            P("sub", None),
            P("sub", None),
        ),
        out_specs=(P("sub", "harm", None, None), P("sub", "harm", None, None)),
        check_vma=False,
    )
```

profile of v0, /device:TPU:1, one launch (start us, length us, event | category | flops | bytes accessed | tf_op | source)
XLA Modules:
  0.0 810.1 jit_solution(11773771976111739545)
XLA Ops:
  0.6 14.5 %collective-permute-start.1 = (f32[1,1,12,64,256]{4,3,2,0,1:T(8,128)}, f32[1,1,12,64,256]{4,3,2,0,1:T(8,128)}, u32[]{:S(2)}, u32[]{:S(2)}) collective-permute-start(f32[1,1,12,64,256]{4,3,2,0,1:T(8,128)} %bitcast.231), channel_id=1, source_target_pairs={{8,0},{16,8},{24,16},{32,24},{40,32},{48,40},{56,48},{64,56},{72,6... | collective-permute-start | bytes 2359304 | tf_op jit(solution)/shard_map/ppermute | solution.py:26
  19.2 12.5 %collective-permute-done.1 = f32[1,1,12,64,256]{4,3,2,0,1:T(8,128)} collective-permute-done((f32[1,1,12,64,256]{4,3,2,0,1:T(8,128)}, f32[1,1,12,64,256]{4,3,2,0,1:T(8,128)}, u32[]{:S(2)}, u32[]{:S(2)}) %collective-permute-start.1) | collective-permute-done | bytes 786464 | tf_op jit(solution)/shard_map/ppermute | solution.py:26
  31.7 7.2 collective-permute-done
  38.9 3.3 maximum_bitcast_fusion
  42.1 3.2 gather_fusion
  46.8 2.3 copy.88
  49.1 6.4 multiply_reduce_fusion.6
  55.5 110.5 %all-reduce.3 = (f32[1,256]{1,0:T(1,128)S(1)}, f32[1,256]{1,0:T(1,128)S(1)}) all-reduce(f32[1,256]{1,0:T(1,128)S(1)} %bitcast.282, f32[1,256]{1,0:T(1,128)S(1)} %bitcast.283), channel_id=1, replica_groups=mesh['sub'=64,'harm'=8] {'sub'}, use_global_device_ids=true, to_apply=%region_1.0 | all-reduce | flops 512 | bytes 4096 | tf_op jit(solution)/shard_map/psum | solution.py:96
  168.2 2.3 copy.89
  170.4 3.5 collective-permute-start.3
  176.1 8.0 collective-permute-done.3
  184.0 6.2 collective-permute-done.2
  190.3 2.7 maximum_bitcast_fusion.1
  193.0 3.2 gather_fusion.1
  196.2 2.3 copy.93
  200.8 3.1 multiply_reduce_fusion.4
  203.9 111.5 %all-reduce.2 = (f32[1,256]{1,0:T(1,128)S(1)}, f32[1,256]{1,0:T(1,128)S(1)}) all-reduce(f32[1,256]{1,0:T(1,128)S(1)} %bitcast.277, f32[1,256]{1,0:T(1,128)S(1)} %bitcast.276), channel_id=1, replica_groups=mesh['sub'=64,'harm'=8] {'sub'}, use_global_device_ids=true, to_apply=%region_5.0 | all-reduce | flops 512 | bytes 4096 | tf_op jit(solution)/shard_map/psum | solution.py:96
  315.5 3.3 multiply_subtract_fusion.3
  318.7 2.3 copy.95
  323.6 61.7 %all-to-all-start = ((f32[1,256,256]{1,0,2:T(1,128)}), f32[1,256,256]{1,0,2:T(1,128)S(1)}, u32[]{:S(2)}, u32[]{:S(2)}) async-start(f32[1,256,256]{1,0,2:T(1,128)} %copy.96), calls=%async_computation | async-start | bytes 524288 | tf_op jit(solution)/shard_map/all_to_all | solution.py:68
  385.3 6.5 all-to-all-done
  396.5 4.4 all-to-all-start.1
  402.1 2.3 copy.94
  404.4 3.0 all-to-all-done.1
  411.6 2.3 scatter_fusion
  413.9 5.9 fusion.27
  421.1 3.6 collective-permute-start.5
  426.7 14.9 %collective-permute-done.5 = f32[1,1,12,64,256]{4,3,2,0,1:T(8,128)S(1)} collective-permute-done((f32[1,1,12,64,256]{4,3,2,0,1:T(8,128)S(1)}, f32[1,1,12,64,256]{4,3,2,0,1:T(8,128)S(1)}, u32[]{:S(2)}, u32[]{:S(2)}) %collective-permute-start.5) | collective-permute-done | bytes 786464 | tf_op jit(solution)/shard_map/ppermute | solution.py:26
  441.6 6.1 collective-permute-done.4
  449.4 3.3 gather_fusion.3
  452.6 2.3 copy.107
  457.0 3.1 multiply_reduce_fusion.2
  460.1 110.9 %all-reduce.1 = (f32[1,256]{1,0:T(1,128)S(1)}, f32[1,256]{1,0:T(1,128)S(1)}) all-reduce(f32[1,256]{1,0:T(1,128)S(1)} %bitcast.279, f32[1,256]{1,0:T(1,128)S(1)} %bitcast.278), channel_id=1, replica_groups=mesh['sub'=64,'harm'=8] {'sub'}, use_global_device_ids=true, to_apply=%region_10.0 | all-reduce | flops 512 | bytes 4096 | tf_op jit(solution)/shard_map/psum | solution.py:96
  573.7 3.1 collective-permute-start.7
  576.7 2.4 collective-permute-start.6
  579.2 2.3 copy.108
  581.5 5.3 collective-permute-done.7
  586.8 6.4 collective-permute-done.6
  593.2 3.3 maximum_bitcast_fusion.3
  596.5 3.2 gather_fusion.4
  599.6 2.3 copy.113
  604.0 3.1 multiply_reduce_fusion
  607.1 111.9 %all-reduce = (f32[1,256]{1,0:T(1,128)S(1)}, f32[1,256]{1,0:T(1,128)S(1)}) all-reduce(f32[1,256]{1,0:T(1,128)S(1)} %bitcast.281, f32[1,256]{1,0:T(1,128)S(1)} %bitcast.280), channel_id=1, replica_groups=mesh['sub'=64,'harm'=8] {'sub'}, use_global_device_ids=true, to_apply=%region_14.0 | all-reduce | flops 512 | bytes 4096 | tf_op jit(solution)/shard_map/psum | solution.py:96
  719.1 3.3 multiply_subtract_fusion
  724.5 66.3 %all_to_all.69 = f32[1,256,256]{1,0,2:T(1,128)S(1)} all-to-all(f32[1,256,256]{1,0,2:T(1,128)S(1)} %copy.116), channel_id=1, replica_groups=mesh['sub'=64,'harm'=8] {'harm'}, dimensions={2} | all-to-all | bytes 524288 | tf_op jit(solution)/shard_map/all_to_all | solution.py:68
  795.5 4.4 all-to-all-start.3
  801.1 5.3 all-to-all-done.3
  807.8 2.3 scatter_fusion.1
  (73 shorter events, 46.0 us)
Async XLA Ops:
  0.6 48.5 %copy-start = (f32[1,1,768,768]{3,2,1,0:T(8,128)S(1)}, f32[1,1,768,768]{3,2,1,0:T(8,128)}, u32[]{:S(2)}) copy-start(f32[1,1,768,768]{3,2,1,0:T(8,128)} %param.6) | copy-start | bytes 7077892
  0.6 31.1 %collective-permute-start.1 = (f32[1,1,12,64,256]{4,3,2,0,1:T(8,128)}, f32[1,1,12,64,256]{4,3,2,0,1:T(8,128)}, u32[]{:S(2)}, u32[]{:S(2)}) collective-permute-start(f32[1,1,12,64,256]{4,3,2,0,1:T(8,128)} %bitcast.231), channel_id=1, source_target_pairs={{8,0},{16,8},{24,16},{32,24},{40,32},{48,40},{56,48},{64,56},{72,6... | collective-permute-start | bytes 2359304 | tf_op jit(solution)/shard_map/ppermute | solution.py:26
  15.2 23.7 %collective-permute-start = (f32[1,1,12,64,256]{4,3,2,0,1:T(8,128)}, f32[1,1,12,64,256]{4,3,2,0,1:T(8,128)}, u32[]{:S(2)}, u32[]{:S(2)}) collective-permute-start(f32[1,1,12,64,256]{4,3,2,0,1:T(8,128)} %bitcast.232), channel_id=1, source_target_pairs={{0,8},{8,16},{16,24},{24,32},{32,40},{40,48},{48,56},{56,64},{64,7... | collective-permute-start | bytes 2359304 | tf_op jit(solution)/shard_map/ppermute | solution.py:24
  55.5 120.5 %copy-start.7 = (s32[1,4]{1,0:T(1,128)S(1)}, s32[1,4]{1,0:T(1,128)}, u32[]{:S(2)}) copy-start(s32[1,4]{1,0:T(1,128)} %param.10) | copy-start | bytes 52
  170.4 13.6 %collective-permute-start.3 = (f32[1,1,12,64,256]{4,3,2,0,1:T(8,128)}, f32[1,1,12,64,256]{4,3,2,0,1:T(8,128)S(1)}, u32[]{:S(2)}, u32[]{:S(2)}) collective-permute-start(f32[1,1,12,64,256]{4,3,2,0,1:T(8,128)} %bitcast.240), channel_id=1, source_target_pairs={{8,0},{16,8},{24,16},{32,24},{40,32},{48,40},{56,48},{64,56},{72,6... | collective-permute-start | bytes 2359304 | tf_op jit(solution)/shard_map/ppermute | solution.py:26
  173.9 16.4 %collective-permute-start.2 = (f32[1,1,12,64,256]{4,3,2,0,1:T(8,128)}, f32[1,1,12,64,256]{4,3,2,0,1:T(8,128)S(1)}, u32[]{:S(2)}, u32[]{:S(2)}) collective-permute-start(f32[1,1,12,64,256]{4,3,2,0,1:T(8,128)} %bitcast.241), channel_id=1, source_target_pairs={{0,8},{8,16},{16,24},{24,32},{32,40},{40,48},{48,56},{56,64},{64,7... | collective-permute-start | bytes 2359304 | tf_op jit(solution)/shard_map/ppermute | solution.py:24
  199.9 0.9 copy-start.4
  323.6 68.2 %all-to-all-start = ((f32[1,256,256]{1,0,2:T(1,128)}), f32[1,256,256]{1,0,2:T(1,128)S(1)}, u32[]{:S(2)}, u32[]{:S(2)}) async-start(f32[1,256,256]{1,0,2:T(1,128)} %copy.96), calls=%async_computation | async-start | bytes 524288 | tf_op jit(solution)/shard_map/all_to_all | solution.py:68
  394.2 7.1 copy-start.6
  396.5 10.9 %all-to-all-start.1 = ((f32[8,256,32]{1,2,0:T(8,128)}), f32[8,256,32]{1,2,0:T(8,128)S(1)}, u32[]{:S(2)}, u32[]{:S(2)}) async-start(f32[8,256,32]{1,2,0:T(8,128)} %copy.101), calls=%async_computation.1 | async-start | bytes 524288 | tf_op jit(solution)/shard_map/all_to_all | solution.py:72
  421.1 20.5 %collective-permute-start.5 = (f32[1,1,12,64,256]{4,3,2,0,1:T(8,128)S(1)}, f32[1,1,12,64,256]{4,3,2,0,1:T(8,128)S(1)}, u32[]{:S(2)}, u32[]{:S(2)}) collective-permute-start(f32[1,1,12,64,256]{4,3,2,0,1:T(8,128)S(1)} %bitcast.246), channel_id=1, source_target_pairs={{8,0},{16,8},{24,16},{32,24},{40,32},{48,40},{56,48},{64,56},{72,6... | collective-permute-start | bytes 2359304 | tf_op jit(solution)/shard_map/ppermute | solution.py:26
  424.8 23.0 %collective-permute-start.4 = (f32[1,1,12,64,256]{4,3,2,0,1:T(8,128)S(1)}, f32[1,1,12,64,256]{4,3,2,0,1:T(8,128)S(1)}, u32[]{:S(2)}, u32[]{:S(2)}) collective-permute-start(f32[1,1,12,64,256]{4,3,2,0,1:T(8,128)S(1)} %bitcast.247), channel_id=1, source_target_pairs={{0,8},{8,16},{16,24},{24,32},{32,40},{40,48},{48,56},{56,64},{64,7... | collective-permute-start | bytes 2359304 | tf_op jit(solution)/shard_map/ppermute | solution.py:24
  449.4 5.5 copy-start.1
  456.1 0.9 copy-start.2
  573.7 13.1 %collective-permute-start.7 = (f32[1,1,12,64,256]{4,3,2,0,1:T(8,128)}, f32[1,1,12,64,256]{4,3,2,0,1:T(8,128)}, u32[]{:S(2)}, u32[]{:S(2)}) collective-permute-start(f32[1,1,12,64,256]{4,3,2,0,1:T(8,128)} %bitcast.243), channel_id=1, source_target_pairs={{8,0},{16,8},{24,16},{32,24},{40,32},{48,40},{56,48},{64,56},{72,6... | collective-permute-start | bytes 2359304 | tf_op jit(solution)/shard_map/ppermute | solution.py:26
  576.7 16.5 %collective-permute-start.6 = (f32[1,1,12,64,256]{4,3,2,0,1:T(8,128)}, f32[1,1,12,64,256]{4,3,2,0,1:T(8,128)}, u32[]{:S(2)}, u32[]{:S(2)}) collective-permute-start(f32[1,1,12,64,256]{4,3,2,0,1:T(8,128)} %bitcast.244), channel_id=1, source_target_pairs={{0,8},{8,16},{16,24},{24,32},{32,40},{40,48},{48,56},{56,64},{64,7... | collective-permute-start | bytes 2359304 | tf_op jit(solution)/shard_map/ppermute | solution.py:24
  603.1 0.9 copy-start.3
  793.3 6.6 copy-start.5
  795.5 10.9 %all-to-all-start.3 = ((f32[8,256,32]{1,2,0:T(8,128)}), f32[8,256,32]{1,2,0:T(8,128)S(1)}, u32[]{:S(2)}, u32[]{:S(2)}) async-start(f32[8,256,32]{1,2,0:T(8,128)} %copy.121), calls=%async_computation.3 | async-start | bytes 524288 | tf_op jit(solution)/shard_map/all_to_all | solution.py:72
where the time goes:
time: 812 us; the launch traced here: 810 us
  blocking collectives  511 us (63%)
  starting transfers between devices  103 us (13%)
  waiting for transfers between devices  81.4 us (10%)
  local copies, waits for them, and re-layouts  49.5 us (6%)
  other arithmetic  34.6 us (4%)
  matrix products  29 us (4%)
    psum x4, blocking collectives, per_device(): lax.psum((jnp.sum(jump * jump, axis=1), jnp.sum(jump * flex_image, axis=1...  445 us
    all_to_all x1, blocking collectives, contact_cycle(): lax.all_to_all(contact_coef, 'harm', split_axis=2, concat_axis=0, tiled=T...  66.3 us
    all_to_all x1, starting transfers between devices, contact_cycle(): lax.all_to_all(contact_coef, 'harm', split_axis=2, concat_axis=0, tiled=T...  61.7 us
    ppermute x4, waiting for transfers between devices, extended(): lax.ppermute(head, axis, [((i + 1) % count, i) for i in range(count)])  40.7 us
    ppermute x4, waiting for transfers between devices, extended(): lax.ppermute(tail, axis, [(i, (i + 1) % count) for i in range(count)])  25.9 us
    ppermute x4, starting transfers between devices, extended(): lax.ppermute(head, axis, [((i + 1) % count, i) for i in range(count)])  24.7 us
    dot_general x5, matrix products, apply_flex(): return jnp.einsum('hij,hjc->hic', flex, field, precision=precise)  21.6 us
  transfers between devices with their start and end apart: 11, of which 11 were waited for; matrix products, arithmetic and copies ran while one was open for 1% of the time, Pallas kernels for 0%

commit v1 on v0

v1 whole, which is shorter than its diff:
```python
import functools
import math

import jax
import jax.numpy as jnp
from jax import lax
from jax.experimental import pallas as pl
from jax.experimental.pallas import tpu as pltpu
from jax.sharding import PartitionSpec as P

MESH = pl.DeviceIdType.MESH
TIMES = 64
ROUNDS = 2
TINY = 1e-6
NB = 12
BLK = 64
ROWS = NB * BLK
COLS = 256
MAXB = 4
CB = 4
CROWS = CB * BLK
NY = 4
CHUNKS = 2
TILE = 384

f32 = jnp.float32
bf16 = jnp.bfloat16


def dot(a, b):
    return jnp.dot(a, b, preferred_element_type=f32)


def split(x):
    high = x.astype(bf16)
    return high, (x - high.astype(f32)).astype(bf16)


def split3(x):
    high = x.astype(bf16)
    rest = x - high.astype(f32)
    middle = rest.astype(bf16)
    return high, middle, (rest - middle.astype(f32)).astype(bf16)


def contact_law(cos_coef, sin_coef, harms):
    half = TIMES // 2
    cos_out = [None] * harms
    sin_out = [None] * harms

    def add(out, k, value, factor):
        if abs(factor) > 1e-9:
            term = value * factor
            out[k] = term if out[k] is None else out[k] + term

    def total(coefs, table, parity):
        result = None
        for k in range(harms):
            if (k + 1) % 2 == parity and abs(table[k]) > 1e-9:
                term = coefs[k] * table[k]
                result = term if result is None else result + term
        return jnp.zeros_like(coefs[0]) if result is None else result

    def cubes(even, odd):
        even2, odd2 = even * even, odd * odd
        return even * (even2 + 3.0 * odd2), odd * (odd2 + 3.0 * even2)

    for t in range(TIMES // 4 + 1):
        cos_t = [math.cos(2 * math.pi * t * (k + 1) / TIMES) for k in range(harms)]
        sin_t = [math.sin(2 * math.pi * t * (k + 1) / TIMES) for k in range(harms)]
        pe, po = total(cos_coef, cos_t, 0), total(cos_coef, cos_t, 1)
        qe, qo = total(sin_coef, sin_t, 0), total(sin_coef, sin_t, 1)
        u1, d1 = cubes(pe + po, qe + qo)
        scale = 2.0 * 2.0 / TIMES
        if t == 0:
            scale *= 0.5
        if t == TIMES // 4:
            scale *= 0.5
        u2, d2 = cubes(pe - po, qo - qe)
        up, um, dp, dm = u1 + u2, u1 - u2, d1 + d2, d1 - d2
        for k in range(harms):
            even = (k + 1) % 2 == 0
            add(cos_out, k, up if even else um, scale * cos_t[k])
            add(sin_out, k, dm if even else dp, scale * sin_t[k])
    return cos_out, sin_out


def kernel(nz, harms, side, partner, cblk, stiff, flex, loads, mult, force, *scratch):
    names = iter(scratch)
    nch = CHUNKS
    width = COLS // nch
    part = CROWS // harms
    flex_v, fh, fl, ld, tr, im, gg, jj, dv, mm, xh, xl, cf, stc, perm, perm_t, tab = (
        next(names) for _ in range(17)
    )
    grid = lambda n: [[next(names) for _ in range(nch)] for _ in range(n)]
    snd, rcv = grid(2 * ROUNDS), grid(2 * ROUNDS)
    sum_y, sum_z = grid(ROUNDS), grid(ROUNDS)
    ct, rc, oc, bc = grid(ROUNDS), grid(ROUNDS), grid(ROUNDS), grid(ROUNDS)
    in_sem, out_sem, ex_s, ex_r, y_s, y_r, z_s, z_r, a_s, a_r = names

    sub = lax.axis_index("sub")
    harm = lax.axis_index("harm")
    subs = nz * NY
    my_y = lax.rem(sub, NY)
    my_z = sub // NY
    right = (lax.rem(sub + 1, subs), harm)
    left = (lax.rem(sub + subs - 1, subs), harm)
    y_peers = [my_z * NY + lax.rem(my_y + d, NY) for d in range(1, NY)]
    z_order = sorted(range(1, nz), key=lambda d: -min(d, nz - d))
    z_peers = {d: lax.rem(my_z + d, nz) * NY + my_y for d in z_order}
    h_order = sorted(range(1, harms), key=lambda d: -min(d, harms - d))
    h_peers = {d: lax.rem(harm + d, harms) for d in h_order}

    barrier = pltpu.get_barrier_semaphore()
    greet = [right, left]
    greet += [(p, harm) for p in y_peers] + [(z_peers[d], harm) for d in z_order]
    greet += [(sub, h_peers[d]) for d in h_order]
    for peer in greet:
        pl.semaphore_signal(barrier, inc=1, device_id=peer, device_id_type=MESH)

    in_copies = [
        pltpu.make_async_copy(loads.at[:, :, pl.ds(c * width, width)], ld.at[c], in_sem.at[c])
        for c in range(nch)
    ]
    in_copies.append(pltpu.make_async_copy(flex, flex_v, in_sem.at[nch]))
    for copy in in_copies:
        copy.start()

    sides = [side[0, b] for b in range(NB)]
    partners = [partner[0, b] for b in range(NB)]
    contacts = [cblk[0, q] for q in range(CB)]
    for way, sign in enumerate((1, -1)):
        count = jnp.int32(0)
        picks = [jnp.int32(0)] * MAXB
        for b in range(NB):
            hit = sides[b] == sign
            picks = [jnp.where(hit & (count == k), b, picks[k]) for k in range(MAXB)]
            count = count + jnp.where(hit, 1, 0)
        for k in range(MAXB):
            tab[4, way * MAXB + k] = picks[k]
    for b in range(NB):
        slot = jnp.int32(0)
        for other in range(NB):
            if other != b:
                before = (sides[other] == sides[b]) & (partners[other] < partners[b])
                slot = slot + jnp.where(before, 1, 0)
        slot = jnp.minimum(slot, MAXB - 1)
        slot = jnp.where(sides[b] == 1, slot + MAXB, slot)
        tab[0, b] = slot
        tab[1, b] = jnp.where(sides[b] != 0, 1, 0)
        place = jnp.int32(0)
        found = jnp.int32(0)
        for q in range(CB):
            same = contacts[q] == b
            place = jnp.where(same, q, place)
            found = jnp.where(same, 1, found)
        tab[2, b] = place
        tab[3, b] = found

    row = lax.broadcasted_iota(jnp.int32, (COLS, COLS), 0)
    col = lax.broadcasted_iota(jnp.int32, (COLS, COLS), 1)
    place = lambda a: 128 * (a % 2) + 64 * (a // 128) + (a % 128) // 2
    perm[...] = jnp.where(place(row) == col, 1.0, 0.0).astype(bf16)
    perm_t[...] = jnp.where(place(col) == row, 1.0, 0.0).astype(bf16)
    column = jnp.sum(jnp.where(row == col, stiff[...], 0.0), axis=1, keepdims=True)
    stc[...] = jnp.broadcast_to(column, (CROWS, width))

    for copy in in_copies:
        copy.wait()

    @pl.loop(0, NB)
    def _(b):
        rows = pl.ds(pl.multiple_of(b * BLK, BLK), BLK)
        fh[rows, :], fl[rows, :] = split(flex_v[rows, :])

    pl.semaphore_wait(barrier, len(greet))

    def exchange(e, c, way):
        peer = right if way == 0 else left
        return pltpu.make_async_remote_copy(
            src_ref=snd[e][c].at[pl.ds(way * MAXB, MAXB)],
            dst_ref=rcv[e][c].at[pl.ds(way * MAXB, MAXB)],
            send_sem=ex_s.at[e, c, way],
            recv_sem=ex_r.at[e, c, way],
            device_id=peer,
            device_id_type=MESH,
        )

    def send_blocks(e, c, source):
        for way in range(2):
            for k in range(way * MAXB, (way + 1) * MAXB):
                snd[e][c][k] = source[c, tab[4, k]]
            exchange(e, c, way).start()

    def fold(x):
        return jnp.sum(x.reshape(BLK // 8, 8, width), axis=0)

    def difference(e, c, source, target):
        for way in range(2):
            exchange(e, c, way).wait_recv()

        def step(b, acc):
            value = source[c, b] - rcv[e][c][tab[0, b]]
            value = jnp.where(tab[1, b] != 0, value, 0.0)
            target[c, b] = value
            xh[c, b], xl[c, b] = split(value)
            return acc + fold(value * value)

        acc = lax.fori_loop(0, NB, step, jnp.zeros((8, width), f32))
        return jnp.sum(acc, axis=0, keepdims=True)

    def product(c, target, subtract=False):
        high = xh[c].reshape(ROWS, width)
        low = xl[c].reshape(ROWS, width)
        count = TILE // BLK

        @pl.loop(0, ROWS // TILE)
        def _(i):
            rows = pl.ds(pl.multiple_of(i * TILE, TILE), TILE)
            blocks = pl.ds(i * count, count)
            first = fh[rows, :]
            out = dot(first, high) + (dot(first, low) + dot(fl[rows, :], high))
            out = out.reshape(count, BLK, width)
            target[c, blocks] = target[c, blocks] - out if subtract else out

    def inner(c, one, two):
        def step(b, acc):
            return acc + fold(one[c, b] * two[c, b])

        acc = lax.fori_loop(0, NB, step, jnp.zeros((8, width), f32))
        return jnp.sum(acc, axis=0, keepdims=True)

    def y_copy(r, c, d):
        ref = sum_y[r][c].at[my_y]
        return pltpu.make_async_remote_copy(
            src_ref=ref,
            dst_ref=ref,
            send_sem=y_s.at[r, c, d],
            recv_sem=y_r.at[r, c, d],
            device_id=(y_peers[d - 1], harm),
            device_id_type=MESH,
        )

    def z_copy(r, c, d):
        ref = sum_z[r][c].at[my_z]
        return pltpu.make_async_remote_copy(
            src_ref=ref,
            dst_ref=ref,
            send_sem=z_s.at[r, c, d],
            recv_sem=z_r.at[r, c, d],
            device_id=(z_peers[d], harm),
            device_id_type=MESH,
        )

    def rows_of(index):
        return pl.ds(pl.multiple_of(index * part, part), part)

    def to_harm(r, c, d):
        return pltpu.make_async_remote_copy(
            src_ref=ct[r][c].at[rows_of(h_peers[d])],
            dst_ref=rc[r][c].at[harm],
            send_sem=a_s.at[r, c, 0, d],
            recv_sem=a_r.at[r, c, 0, d],
            device_id=(sub, h_peers[d]),
            device_id_type=MESH,
        )

    def from_harm(r, c, d):
        return pltpu.make_async_remote_copy(
            src_ref=oc[r][c].at[h_peers[d]],
            dst_ref=bc[r][c].at[rows_of(harm)],
            send_sem=a_s.at[r, c, 1, d],
            recv_sem=a_r.at[r, c, 1, d],
            device_id=(sub, h_peers[d]),
            device_id_type=MESH,
        )

    def contact(r, c):
        strips = part // (8 * nch)

        def piece(k, i):
            both = [
                rc[r][c][k, pl.ds(pl.multiple_of((i + n * strips) * 8, 8), 8), :]
                for n in range(nch)
            ]
            return jnp.concatenate(both, axis=1) if nch > 1 else both[0]

        @pl.loop(0, strips)
        def _(i):
            rows = jnp.concatenate([piece(k, i) for k in range(harms)], axis=0)
            high, middle, low = split3(rows)
            p = perm[...]
            flat = dot(high, p) + (dot(middle, p) + dot(low, p))
            cos_coef = [flat[8 * k : 8 * k + 8, :128] for k in range(harms)]
            sin_coef = [flat[8 * k : 8 * k + 8, 128:] for k in range(harms)]
            cos_out, sin_out = contact_law(cos_coef, sin_coef, harms)
            flat = jnp.concatenate(
                [jnp.concatenate(cos_out, axis=0), jnp.concatenate(sin_out, axis=0)], axis=1
            )
            high, middle, low = split3(flat)
            p = perm_t[...]
            rows = dot(high, p) + (dot(middle, p) + dot(low, p))
            for k in range(harms):
                for n in range(nch):
                    place = pl.ds(pl.multiple_of((i + n * strips) * 8, 8), 8)
                    oc[r][c][k, place, :] = rows[8 * k : 8 * k + 8, n * width : (n + 1) * width]

    chunks = range(nch)
    lanes = [pl.ds(c * width, width) for c in chunks]
    halves = width // 128

    for c in chunks:
        send_blocks(0, c, ld)

    for r in range(ROUNDS):
        source = ld if r == 0 else tr
        sums = {}
        for c in chunks:
            square = difference(2 * r, c, source, jj)
            product(c, im)
            send_blocks(2 * r + 1, c, im)
            sums[c] = [square, inner(c, jj, im)]
        for c in chunks:
            square = difference(2 * r + 1, c, im, dv)
            product(c, gg)
            sums[c] += [square, inner(c, dv, gg)]
            for n in range(halves):
                for i in range(4):
                    piece = sums[c][i][:, n * 128 : (n + 1) * 128]
                    sum_y[r][c][my_y, pl.ds(4 * n + i, 1), :] = piece
            for d in range(1, NY):
                y_copy(r, c, d).start()
        for c in chunks:
            for d in range(1, NY):
                y_copy(r, c, d).wait_recv()
            total = sum_y[r][c][0]
            for d in range(1, NY):
                total = total + sum_y[r][c][d]
            sum_z[r][c][my_z] = total
            for d in z_order:
                z_copy(r, c, d).start()
        for c in chunks:
            for d in z_order:
                z_copy(r, c, d).wait_recv()
            total = jnp.sum(sum_z[r][c][...], axis=0)
            square, curve, square_d, curve_d = [
                jnp.concatenate([total[4 * n + i : 4 * n + i + 1] for n in range(halves)], axis=1)
                for i in range(4)
            ]
            first = square / (curve + TINY)
            square = square - 4.0 * first * curve + first * first * square_d
            curve = curve - first * square_d + first * first * curve_d
            second = square / (curve + TINY)
            both, cross = first + second, first * second
            for q in range(CB):
                b = cblk[0, q]
                value = source[c, b] - both * im[c, b] + cross * gg[c, b]
                ct[r][c][pl.ds(q * BLK, BLK), :] = value
            for d in h_order:
                to_harm(r, c, d).start()
            rc[r][c][harm] = ct[r][c][rows_of(harm), :]

            @pl.loop(0, NB)
            def _(b):
                change = cross * dv[c, b] - both * jj[c, b]
                mm[c, b] = change if r == 0 else mm[c, b] + change
                if r + 1 < ROUNDS:
                    tr[c, b] = source[c, b] - both * im[c, b] + cross * gg[c, b]

        for c in chunks:
            for d in h_order:
                to_harm(r, c, d).wait_recv()
            contact(r, c)
            for d in h_order:
                from_harm(r, c, d).start()
            bc[r][c][rows_of(harm), :] = oc[r][c][harm]
        for c in chunks:
            for d in h_order:
                from_harm(r, c, d).wait_recv()
            for q in range(CB):
                rows = pl.ds(q * BLK, BLK)
                cf[c, q] = bc[r][c][rows, :] * stc[rows, :]

            @pl.loop(0, NB)
            def _(b):
                value = jnp.where(tab[3, b] != 0, cf[c, tab[2, b]], 0.0)
                mm[c, b] = mm[c, b] - value
                if r + 1 < ROUNDS:
                    xh[c, b], xl[c, b] = split(value)

            if r + 1 < ROUNDS:
                product(c, tr, subtract=True)
                send_blocks(2 * r + 2, c, tr)
            else:
                pltpu.make_async_copy(mm.at[c], mult.at[:, :, lanes[c]], out_sem.at[c, 0]).start()
                pltpu.make_async_copy(cf.at[c], force.at[:, :, lanes[c]], out_sem.at[c, 1]).start()

    for c in chunks:
        for r in range(ROUNDS):
            for way in range(2):
                exchange(2 * r, c, way).wait_send()
                exchange(2 * r + 1, c, way).wait_send()
            for d in range(1, NY):
                y_copy(r, c, d).wait_send()
            for d in z_order:
                z_copy(r, c, d).wait_send()
            for d in h_order:
                to_harm(r, c, d).wait_send()
                from_harm(r, c, d).wait_send()
        pltpu.make_async_copy(mm.at[c], mult.at[:, :, lanes[c]], out_sem.at[c, 0]).wait()
        pltpu.make_async_copy(cf.at[c], force.at[:, :, lanes[c]], out_sem.at[c, 1]).wait()


def per_device(flex, loads, side, partner, contact_blocks, contact_stiff):
    harms = lax.axis_size("harm")
    nz = lax.axis_size("sub") // NY
    nch = CHUNKS
    width = COLS // nch
    part = CROWS // harms
    sums = 4 * (width // 128)
    field = pltpu.VMEM((nch, NB, BLK, width), f32)
    field16 = pltpu.VMEM((nch, NB, BLK, width), bf16)
    scratch = [
        pltpu.VMEM((ROWS, ROWS), f32),
        pltpu.VMEM((ROWS, ROWS), bf16),
        pltpu.VMEM((ROWS, ROWS), bf16),
    ]
    scratch += [field] * 7 + [field16] * 2
    scratch += [
        pltpu.VMEM((nch, CB, BLK, width), f32),
        pltpu.VMEM((CROWS, width), f32),
        pltpu.VMEM((COLS, COLS), bf16),
        pltpu.VMEM((COLS, COLS), bf16),
        pltpu.SMEM((5, NB), jnp.int32),
    ]
    grid = lambda n, shape: [pltpu.VMEM(shape, f32)] * (n * nch)
    scratch += grid(2 * ROUNDS, (2 * MAXB, BLK, width)) * 2
    scratch += grid(ROUNDS, (NY, sums, 128)) + grid(ROUNDS, (nz, sums, 128))
    scratch += grid(ROUNDS, (CROWS, width)) + grid(ROUNDS, (harms, part, width)) * 2
    scratch += grid(ROUNDS, (CROWS, width))
    sem = pltpu.SemaphoreType.DMA
    scratch += [sem((nch + 1,)), sem((nch, 2))]
    scratch += [sem((2 * ROUNDS, nch, 2))] * 2
    scratch += [sem((ROUNDS, nch, NY))] * 2
    scratch += [sem((ROUNDS, nch, nz))] * 2
    scratch += [sem((ROUNDS, nch, 2, harms))] * 2
    smem = pl.BlockSpec(memory_space=pltpu.SMEM)
    anywhere = pl.BlockSpec(memory_space=pl.ANY)
    mult, force = pl.pallas_call(
        functools.partial(kernel, nz, harms),
        out_shape=(
            jax.ShapeDtypeStruct((NB, BLK, COLS), f32),
            jax.ShapeDtypeStruct((CB, BLK, COLS), f32),
        ),
        in_specs=[smem] * 3 + [pl.BlockSpec(memory_space=pltpu.VMEM)] + [anywhere] * 2,
        out_specs=(anywhere, anywhere),
        scratch_shapes=scratch,
        compiler_params=pltpu.CompilerParams(
            collective_id=0, has_side_effects=True, vmem_limit_bytes=48 << 20
        ),
    )(
        side,
        partner,
        contact_blocks,
        contact_stiff,
        flex.reshape(ROWS, ROWS),
        loads.reshape(NB, BLK, COLS),
    )
    return mult.reshape(loads.shape), force.reshape(1, 1, CROWS, COLS)


def solution(mesh):
    return jax.shard_map(
        per_device,
        mesh=mesh,
        in_specs=(
            P("sub", "harm", None, None),
            P("sub", "harm", None, None),
            P("sub", None),
            P("sub", None),
            P("sub", None),
            P("sub", None),
        ),
        out_specs=(P("sub", "harm", None, None), P("sub", "harm", None, None)),
        check_vma=False,
    )
```

time: 812 us -> 102 us (0.13)
  blocking collectives: 511 us -> 0 us
  starting transfers between devices: 103 us -> 0 us
  Pallas kernels: 0 us -> 94.3 us
  waiting for transfers between devices: 81.4 us -> 0 us
  local copies, waits for them, and re-layouts: 49.5 us -> 7.02 us
  other arithmetic: 34.6 us -> 0 us
  matrix products: 29 us -> 0 us
    psum x4 -> x0, blocking collectives: 445 us -> none  [per_device(): lax.psum((jnp.sum(jump * jump, axis=1), jnp.sum(jump * flex_image, axis=1...]
    pallas_call x0 -> x1, Pallas kernels: none -> 94.3 us  [per_device(): pl.pallas_call(functools.partial(kernel, nz, harms), out_shape=(jax.Shape...]
    all_to_all x3 -> x0, starting transfers between devices: 70.4 us -> none  [the longest x1 61.7 us: contact_cycle(): lax.all_to_all(contact_coef, 'harm', split_axis=2, concat_axis=0, tiled=T...]
    ppermute x8 -> x0, waiting for transfers between devices: 66.7 us -> none  [the longest x4 40.7 us: extended(): lax.ppermute(head, axis, [((i + 1) % count, i) for i in range(count)])]
    all_to_all x1 -> x0, blocking collectives: 66.3 us -> none  [contact_cycle(): lax.all_to_all(contact_coef, 'harm', split_axis=2, concat_axis=0, tiled=T...]
    ppermute x8 -> x0, starting transfers between devices: 33.1 us -> none  [the longest x4 24.7 us: extended(): lax.ppermute(head, axis, [((i + 1) % count, i) for i in range(count)])]
    dot_general x13 -> x0, matrix products: 29 us -> none  [the longest x5 21.6 us: apply_flex(): return jnp.einsum('hij,hjc->hic', flex, field, precision=precise)]
    gather x6 -> x0, local copies, waits for them, and re-layouts: 15 us -> none  [the longest x4 12.8 us: opposite_whole(): picked = jax.vmap(lambda one: one[side + 1, partner], in_axes=1)(padded)]
  transfers between devices with their start and end apart: 11 -> 0, of which waited for: 11 -> 0; matrix products, arithmetic and copies ran while one was open for 1% -> 0% of each run, Pallas kernels for 0% -> 0%
where the time goes in v1:
time: 102 us
  Pallas kernels  94.3 us (92%)
  local copies, waits for them, and re-layouts  7.02 us (7%)
    pallas_call x1, Pallas kernels, per_device(): pl.pallas_call(functools.partial(kernel, nz, harms), out_shape=(jax.Shape...  94.3 us
    unnamed x14, local copies, waits for them, and re-layouts  7.02 us

profile of v1, /device:TPU:1, one launch (start us, length us, event | category | flops | bytes accessed | tf_op | source)
XLA Modules:
  0.0 102.0 jit_solution(10362581865622805262)
XLA Ops:
  0.6 0.0 copy-start
  0.6 1.7 %copy-done = f32[1,1,768,768]{3,2,1,0:T(8,128)S(1)} copy-done((f32[1,1,768,768]{3,2,1,0:T(8,128)S(1)}, f32[1,1,768,768]{3,2,1,0:T(8,128)}, u32[]{:S(2)}) %copy-start) | copy-done | bytes 2359320
  2.3 0.0 copy-start.1
  2.3 1.1 %copy-done.1 = f32[1,1,768,256]{3,2,1,0:T(8,128)S(1)} copy-done((f32[1,1,768,256]{3,2,1,0:T(8,128)S(1)}, f32[1,1,768,256]{3,2,1,0:T(8,128)}, u32[]{:S(2)}) %copy-start.1) | copy-done | bytes 786456
  3.4 0.0 copy-start.2
  3.4 0.7 copy-done.2
  4.1 0.0 copy-start.3
  4.1 0.7 copy-done.3
  4.8 0.0 copy-start.4
  4.8 0.7 copy-done.4
  5.4 0.0 copy-start.5
  5.4 0.7 copy-done.5
  6.1 94.3 %shard_map.77 = (f32[12,64,256]{2,1,0:T(8,128)S(1)}, f32[4,64,256]{2,1,0:T(8,128)S(1)}) custom-call(s32[1,12]{1,0:T(1,128)S(1)} %copy-done.3, s32[1,12]{1,0:T(1,128)S(1)} %copy-done.4, s32[1,4]{1,0:T(1,128)S(1)} %copy-done.5, f32[1,256]{1,0:T(1,128)S(1)} %copy-done.2, f32[768,768]{1,0:T(8,128)S(1)} %bitcast.4, f32[12,64,256]{2,1,0:T(8,128)S(1)} %bitcast.6), custom_call_target="tpu_custom_call" | custom-call | tf_op jit(solution)/shard_map/pallas_call | solution.py:450
  100.4 0.9 copy.10
  101.3 0.7 copy.11
Async XLA Ops:
  0.6 1.7 %copy-start = (f32[1,1,768,768]{3,2,1,0:T(8,128)S(1)}, f32[1,1,768,768]{3,2,1,0:T(8,128)}, u32[]{:S(2)}) copy-start(f32[1,1,768,768]{3,2,1,0:T(8,128)} %param.6) | copy-start | bytes 7077892
  2.3 1.1 %copy-start.1 = (f32[1,1,768,256]{3,2,1,0:T(8,128)S(1)}, f32[1,1,768,256]{3,2,1,0:T(8,128)}, u32[]{:S(2)}) copy-start(f32[1,1,768,256]{3,2,1,0:T(8,128)} %param.7) | copy-start | bytes 2359300
  3.4 0.7 copy-start.2
  4.1 0.7 copy-start.3
  4.8 0.7 copy-start.4
  5.4 0.7 copy-start.5

commit v2 on v0

v2 whole, which is shorter than its diff:
```python
import functools
import math

import jax
import jax.numpy as jnp
from jax import lax
from jax.experimental import pallas as pl
from jax.experimental.pallas import tpu as pltpu
from jax.sharding import PartitionSpec as P

MESH = pl.DeviceIdType.MESH
TIMES = 64
ROUNDS = 2
TINY = 1e-6
NB = 12
BLK = 64
ROWS = NB * BLK
COLS = 256
MAXB = 4
CB = 4
CROWS = CB * BLK
NY = 4
NCH = 2
WIDTH = COLS // NCH
S_ROWS = 2 * MAXB * BLK
TILE = 256
PAIRS = ROWS // 128
OUT = pl.BlockSpec(memory_space=pltpu.VMEM)

f32 = jnp.float32
bf16 = jnp.bfloat16


def dot(a, b):
    return jnp.dot(a, b, preferred_element_type=f32)


def split(x):
    high = x.astype(bf16)
    return high, (x - high.astype(f32)).astype(bf16)


def cube_law(coefs, table, odd_lane):
    harms = len(coefs)
    out = [None] * harms

    def plus(x, y):
        return y if x is None else x + y

    def cubes(y):
        square = y * y
        turned = pltpu.roll(square, 127, axis=2), pltpu.roll(square, 1, axis=2)
        return y * (square + 3.0 * jnp.where(odd_lane, turned[1], turned[0]))

    for t in range(TIMES // 4 + 1):
        parity = [None, None]
        for k in range(harms):
            parity[(k + 1) % 2] = plus(parity[(k + 1) % 2], coefs[k] * table[t, k])
        first, second = cubes(parity[0] + parity[1]), cubes(parity[0] - parity[1])
        both = [first + second, first - second]
        if t in (0, TIMES // 4):
            both = [0.5 * x for x in both]
        for k in range(harms):
            out[k] = plus(out[k], both[(k + 1) % 2] * table[t, k])
    return [(4.0 / TIMES) * x for x in out]


def relay_steps(nz):
    radius, steps = min(2, nz // 2), []
    while radius < nz // 2:
        steps.append(radius)
        radius *= 2
    return steps


def drain(ref, sem):
    pltpu.make_async_copy(ref, ref, sem).wait()


def signal(sem, peer):
    pl.semaphore_signal(sem, inc=1, device_id=peer, device_id_type=MESH)


def kernel(nz, harms, side_h, partner_h, cblk_h, stiff_h, flex_h, loads_h, mult, force, *scratch):
    names = iter(scratch)
    take = lambda n: [next(names) for _ in range(n)]
    side, partner, cblk, tab = take(4)
    stiff, flex, loads, fh, fl, x2, stc, waves = take(8)
    js, ds, gs, tn, ms = (take(NCH) for _ in range(5))
    imc, gc, tc, old, mo = (take(NCH) for _ in range(5))
    snd = [take(NCH) for _ in range(2 * ROUNDS)]
    rcv = [take(NCH) for _ in range(2 * ROUNDS)]
    sum_y, sum_z, ct, rc, oc, bc = ([take(NCH) for _ in range(ROUNDS)] for _ in range(6))
    in_sem, ex_s, ex_r, y_s, y_r, z_s, z_r, a_s, a_r = take(9)
    told = take(len(relay_steps(nz)))

    part = CROWS // harms
    sub = lax.axis_index("sub")
    harm = lax.axis_index("harm")
    subs = nz * NY
    my_y = lax.rem(sub, NY)
    my_z = sub // NY
    right = (lax.rem(sub + 1, subs), harm)
    left = (lax.rem(sub + subs - 1, subs), harm)
    y_peers = [(my_z * NY + lax.rem(my_y + d, NY), harm) for d in range(1, NY)]
    z_order = sorted(range(1, nz), key=lambda d: -min(d, nz - d))
    z_peers = {d: (lax.rem(my_z + d, nz) * NY + my_y, harm) for d in z_order}
    h_order = sorted(range(1, harms), key=lambda d: -min(d, harms - d))
    h_peers = {d: lax.rem(harm + d, harms) for d in h_order}

    copies = [
        pltpu.make_async_copy(one, two, in_sem.at[i])
        for i, (one, two) in enumerate(
            (
                (side_h, side),
                (partner_h, partner),
                (cblk_h, cblk),
                (loads_h, loads),
                (stiff_h, stiff),
            )
        )
    ]
    copies += [
        pltpu.make_async_copy(
            flex_h.at[:, :, pl.ds(128 * i, 128)], flex.at[i], in_sem.at[len(copies)]
        )
        for i in range(PAIRS)
    ]
    for copy in copies[:3]:
        copy.start()
    barrier = pltpu.get_barrier_semaphore()
    near = [d for d in z_order if min(d, nz - d) <= 2]
    greet = [right, left] + [z_peers[d] for d in near] + y_peers + [(sub, h_peers[d]) for d in h_order]
    for peer in greet:
        signal(barrier, peer)

    for copy in copies[3:]:
        copy.start()
    for copy in copies[:3]:
        copy.wait()

    sides = [side[0, b] for b in range(NB)]
    partners = [partner[0, b] for b in range(NB)]
    contacts = [cblk[0, q] for q in range(CB)]
    one, zero = jnp.int32(1), jnp.int32(0)
    ranks = []
    count_r = count_l = zero
    for b in range(NB):
        rank = zero
        for other in range(NB):
            if other != b:
                before = (sides[other] == -1) & (partners[other] < partners[b])
                rank = rank + jnp.where(before, one, zero)
        is_r, is_l = sides[b] == 1, sides[b] == -1
        slot = jnp.where(is_r, count_r, jnp.where(is_l, MAXB + rank, zero))
        slot = jnp.minimum(slot, 2 * MAXB - 1)
        count_r = count_r + jnp.where(is_r, one, zero)
        count_l = count_l + jnp.where(is_l, one, zero)
        ranks.append(jnp.where(sides[b] != 0, slot, -1))
        tab[2, b] = slot
        tab[3, b] = jnp.where(sides[b] != 0, one, zero)
    for k in range(2 * MAXB):
        block = zero
        for b in range(NB):
            block = jnp.where(ranks[b] == k, b, block)
        tab[0, k] = block
        tab[1, k] = jnp.where(k % MAXB < (count_r if k < MAXB else count_l), one, zero)
    for q in range(CB):
        tab[0, 2 * MAXB + q] = contacts[q]
    def exchange(e, c, way):
        return pltpu.make_async_remote_copy(
            src_ref=snd[e][c].at[pl.ds(way * MAXB, MAXB)],
            dst_ref=rcv[e][c].at[pl.ds((1 - way) * MAXB, MAXB)],
            send_sem=ex_s.at[e, c],
            recv_sem=ex_r.at[e, c],
            device_id=right if way == 0 else left,
            device_id_type=MESH,
        )

    def tell(i):
        steps = relay_steps(nz)
        if i < len(steps):
            signal(told[i], z_peers[steps[i]])
            signal(told[i], z_peers[nz - steps[i]])

    def hear(i):
        if i < len(told):
            pl.semaphore_wait(told[i], 2)
            tell(i + 1)

    def send(e, c):
        for way in range(2):
            exchange(e, c, way).start()

    copies[3].wait()
    lanes = [pl.ds(c * WIDTH, WIDTH) for c in range(NCH)]

    for c in range(NCH):

        @pl.loop(0, 2 * MAXB)
        def _(k):
            snd[0][c][k] = loads[tab[0, k], :, lanes[c]]

    pl.semaphore_wait(barrier, len(greet))
    send(0, 0)
    tell(0)

    for b in range(NB):
        place = found = zero
        for q in range(CB):
            same = contacts[q] == b
            place = jnp.where(same, q, place)
            found = jnp.where(same, one, found)
        tab[4, b] = place
        tab[5, b] = found

    for c in range(NCH):
        for q in range(CB):
            tc[c][q] = loads[cblk[0, q], :, lanes[c]]

    drain(flex, in_sem.at[5])
    lane = lax.broadcasted_iota(jnp.int32, (BLK, 128), 1)

    @pl.loop(0, 2 * MAXB + CB)
    def _(k):
        place = pl.ds(pl.multiple_of(k * BLK, BLK), BLK)

        def half(block, odd):
            pair = lax.div(block, jnp.int32(2))
            value = flex[pair, tab[0, k]]
            turned = pltpu.roll(value, 64, axis=1)
            return jnp.where(block - 2 * pair == odd, value, turned)

        for i in range(PAIRS):
            value = jnp.where(lane < 64, half(tab[0, 2 * i], 0), half(tab[0, 2 * i + 1], 1))
            cols = slice(128 * i, 128 * i + 128)
            fh[place, cols], fl[place, cols] = split(value)

    hear(0)
    drain(snd[0][0], ex_s.at[0, 0])
    send(0, 1)

    odd_lane = lax.broadcasted_iota(jnp.int32, (8, 128), 1) % 2 == 1
    for t in range(TIMES // 4 + 1):
        for k in range(harms):
            angle = 2 * math.pi * t * (k + 1) / TIMES
            waves[t, k] = jnp.where(odd_lane, math.sin(angle), math.cos(angle)).astype(f32)
    copies[4].wait()
    row = lax.broadcasted_iota(jnp.int32, (CROWS, CROWS), 0)
    col = lax.broadcasted_iota(jnp.int32, (CROWS, CROWS), 1)
    column = jnp.sum(jnp.where(row == col, stiff[...], 0.0), axis=1, keepdims=True)
    stc[...] = jnp.broadcast_to(column, (CROWS, WIDTH))

    def fold(x):
        return jnp.sum(x.reshape(BLK // 8, 8, WIDTH), axis=0)

    def put(k, value):
        rows = pl.ds(pl.multiple_of(k * BLK, BLK), BLK)
        x2[rows, :WIDTH], x2[rows, WIDTH:] = split(value)

    def total(acc):
        return jnp.sum(acc, axis=0, keepdims=True)

    def difference(e, c, target):
        def step(k, acc):
            value = snd[e][c][k] - rcv[e][c][k]
            value = jnp.where(tab[1, k] != 0, value, 0.0)
            target[k] = value
            put(k, value)
            return acc + fold(value * value)

        return total(lax.fori_loop(0, 2 * MAXB, step, jnp.zeros((8, WIDTH), f32)))

    def inner(one, two):
        acc = jnp.zeros((8, WIDTH), f32)
        return total(lax.fori_loop(0, 2 * MAXB, lambda k, a: a + fold(one[k] * two[k]), acc))

    def product(rows, cols, target, base=None):
        x = x2[0 : cols[1] - cols[0], :]
        for at in range(rows[0], rows[1], TILE):
            first = fh[at : at + TILE, cols[0] : cols[1]]
            second = fl[at : at + TILE, cols[0] : cols[1]]
            out = dot(first, x) + dot(second, x)
            out = (out[:, :WIDTH] + out[:, WIDTH:]).reshape(TILE // BLK, BLK, WIDTH)
            blocks = pl.ds((at - rows[0]) // BLK, TILE // BLK)
            target[blocks] = out if base is None else base[blocks] - out

    def y_copy(r, c, d):
        ref = sum_y[r][c].at[my_y]
        return pltpu.make_async_remote_copy(
            src_ref=ref,
            dst_ref=ref,
            send_sem=y_s.at[r, c],
            recv_sem=y_r.at[r, c],
            device_id=y_peers[d - 1],
            device_id_type=MESH,
        )

    def z_copy(r, c, d):
        ref = sum_z[r][c].at[my_z]
        return pltpu.make_async_remote_copy(
            src_ref=ref,
            dst_ref=ref,
            send_sem=z_s.at[r, c],
            recv_sem=z_r.at[r, c],
            device_id=z_peers[d],
            device_id_type=MESH,
        )

    def rows_of(index):
        return pl.ds(pl.multiple_of(index * part, part), part)

    def to_harm(r, c, d):
        return pltpu.make_async_remote_copy(
            src_ref=ct[r][c].at[rows_of(h_peers[d])],
            dst_ref=rc[r][c].at[harm],
            send_sem=a_s.at[r, c, 0],
            recv_sem=a_r.at[r, c, 0],
            device_id=(sub, h_peers[d]),
            device_id_type=MESH,
        )

    def from_harm(r, c, d):
        return pltpu.make_async_remote_copy(
            src_ref=oc[r][c].at[h_peers[d]],
            dst_ref=bc[r][c].at[rows_of(harm)],
            send_sem=a_s.at[r, c, 1],
            recv_sem=a_r.at[r, c, 1],
            device_id=(sub, h_peers[d]),
            device_id_type=MESH,
        )

    def contact(r, c):
        odd = jnp.broadcast_to(odd_lane, (2, 8, 128))

        @pl.loop(0, part // 16)
        def _(i):
            rows = pl.ds(pl.multiple_of(i * 16, 16), 16)
            coefs = [rc[r][c][k, rows, :].reshape(2, 8, 128) for k in range(harms)]
            for k, value in enumerate(cube_law(coefs, waves, odd)):
                oc[r][c][k, rows, :] = value.reshape(16, 128)

    shared, joint, every = (0, S_ROWS), (S_ROWS, ROWS), range(NCH)

    def stage_jump(r, c):
        drain(rcv[2 * r][c], ex_r.at[2 * r, c])
        square = difference(2 * r, c, js[c])
        product(shared, shared, snd[2 * r + 1][c])
        send(2 * r + 1, c)
        product(joint, shared, imc[c])
        sum_z[r][c][my_z, 0:1, :] = square
        sum_z[r][c][my_z, 1:2, :] = inner(js[c], snd[2 * r + 1][c])

    def stage_image(r, c):
        drain(rcv[2 * r + 1][c], ex_r.at[2 * r + 1, c])
        square = difference(2 * r + 1, c, ds[c])
        product(shared, shared, gs[c])
        sum_z[r][c][my_z, 2:3, :] = square
        sum_z[r][c][my_z, 3:4, :] = inner(ds[c], gs[c])
        if r == 0 and c == 0:
            hear(1)
            assert len(told) <= 2
        for d in z_order:
            z_copy(r, c, d).start()
        product(joint, shared, gc[c])

    def stage_sums(r, c):
        drain(sum_z[r][c].at[pl.ds(0, nz - 1)], z_r.at[r, c])
        sum_y[r][c][my_y] = jnp.sum(sum_z[r][c][...], axis=0)
        for d in range(1, NY):
            y_copy(r, c, d).start()

    def stage_step(r, c):
        drain(sum_y[r][c].at[pl.ds(0, NY - 1)], y_r.at[r, c])
        value = jnp.sum(sum_y[r][c][...], axis=0)
        square, curve, square_d, curve_d = (value[i : i + 1] for i in range(4))
        first = square / (curve + TINY)
        square = square - 4.0 * first * curve + first * first * square_d
        curve = curve - first * square_d + first * first * curve_d
        second = square / (curve + TINY)
        both, cross = first + second, first * second
        for q in range(CB):
            value = tc[c][q] - both * imc[c][q] + cross * gc[c][q]
            ct[r][c][pl.ds(q * BLK, BLK), :] = value
        for d in h_order:
            to_harm(r, c, d).start()
        rc[r][c][harm] = ct[r][c][rows_of(harm), :]

        @pl.loop(0, 2 * MAXB)
        def _(k):
            change = cross * ds[c][k] - both * js[c][k]
            ms[c][k] = change if r == 0 else ms[c][k] + change
            if r + 1 < ROUNDS:
                image = snd[2 * r + 1][c][k]
                tn[c][k] = snd[2 * r][c][k] - both * image + cross * gs[c][k]

        if r + 1 == ROUNDS:

            @pl.loop(0, NB)
            def _(b):
                value = jnp.where(tab[3, b] != 0, ms[c][tab[2, b]], 0.0)
                mo[c][b] = value - jnp.where(tab[5, b] != 0, old[c][tab[4, b]], 0.0)

    def stage_contact(r, c):
        drain(rc[r][c].at[pl.ds(0, harms - 1)], a_r.at[r, c, 0])
        contact(r, c)
        for d in h_order:
            from_harm(r, c, d).start()
        bc[r][c][rows_of(harm), :] = oc[r][c][harm]

    def stage_force(r, c):
        drain(bc[r][c].at[pl.ds(0, (harms - 1) * part)], a_r.at[r, c, 1])
        for q in range(CB):
            rows = pl.ds(q * BLK, BLK)
            value = bc[r][c][rows, :] * stc[rows, :]
            if r + 1 < ROUNDS:
                old[c][q] = value
                put(q, value)
            else:
                old[c][q] = value
                force[q, :, lanes[c]] = value
        if r + 1 < ROUNDS:
            product(shared, joint, snd[2 * r + 2][c], tn[c])
            send(2 * r + 2, c)
            for q in range(CB):
                tc[c][q] = ct[r][c][pl.ds(q * BLK, BLK), :]
            product(joint, joint, tc[c], tc[c])
        else:

            @pl.loop(0, NB)
            def _(b):
                value = jnp.where(tab[5, b] != 0, old[c][tab[4, b]], 0.0)
                mult[b, :, lanes[c]] = mo[c][b] - value

    def settle(r, c):
        if r > 0 or c > 0:
            drain(snd[2 * r][c], ex_s.at[2 * r, c])
        drain(snd[2 * r + 1][c], ex_s.at[2 * r + 1, c])
        drain(sum_y[r][c].at[pl.ds(0, NY - 1)], y_s.at[r, c])
        drain(sum_z[r][c].at[pl.ds(0, nz - 1)], z_s.at[r, c])
        drain(ct[r][c].at[pl.ds(0, (harms - 1) * part)], a_s.at[r, c, 0])

    def settle_last(r, c):
        drain(oc[r][c].at[pl.ds(0, harms - 1)], a_s.at[r, c, 1])

    for r in range(ROUNDS):
        for c in every:
            stage_jump(r, c)
            if r > 0 and c == NCH - 1:
                for old_c in every:
                    settle(r - 1, old_c)
                    settle_last(r - 1, old_c)
        for c in every:
            stage_image(r, c)
        for c in every:
            stage_sums(r, c)
            if c > 0:
                stage_step(r, c - 1)
        stage_step(r, NCH - 1)
        for c in every:
            stage_contact(r, c)
        if r == ROUNDS - 1:
            for c in every:
                settle(r, c)
        for c in every:
            stage_force(r, c)
    for c in every:
        settle_last(ROUNDS - 1, c)


def per_device(flex, loads, side, partner, contact_blocks, contact_stiff):
    harms = lax.axis_size("harm")
    nz = lax.axis_size("sub") // NY
    part = CROWS // harms
    slots, joint, whole = (
        [pltpu.VMEM((n, BLK, WIDTH), f32)] * NCH for n in (2 * MAXB, CB, NB)
    )
    vmem = lambda *shape: [pltpu.VMEM(shape, f32)] * (NCH * ROUNDS)
    sem = pltpu.SemaphoreType.DMA
    scratch = [
        pltpu.SMEM((1, NB), jnp.int32),
        pltpu.SMEM((1, NB), jnp.int32),
        pltpu.SMEM((1, CB), jnp.int32),
        pltpu.SMEM((6, NB), jnp.int32),
        pltpu.VMEM((1, CROWS), f32),
        pltpu.VMEM((PAIRS, NB, BLK, 128), f32),
        pltpu.VMEM((NB, BLK, COLS), f32),
        pltpu.VMEM((ROWS, ROWS), bf16),
        pltpu.VMEM((ROWS, ROWS), bf16),
        pltpu.VMEM((S_ROWS, 2 * WIDTH), bf16),
        pltpu.VMEM((CROWS, WIDTH), f32),
        pltpu.VMEM((TIMES // 4 + 1, harms, 8, 128), f32),
    ]
    scratch += slots * 5 + joint * 4 + whole
    scratch += slots * (2 * ROUNDS) * 2
    scratch += vmem(NY, 4, WIDTH) + vmem(nz, 4, WIDTH)
    scratch += vmem(CROWS, WIDTH) + vmem(harms, part, WIDTH) * 2 + vmem(CROWS, WIDTH)
    scratch += [sem((6,))]
    scratch += [sem((2 * ROUNDS, NCH))] * 2
    scratch += [sem((ROUNDS, NCH))] * 4
    scratch += [sem((ROUNDS, NCH, 2))] * 2
    scratch += [pltpu.SemaphoreType.REGULAR] * len(relay_steps(nz))
    hbm = pl.BlockSpec(memory_space=pltpu.HBM)
    mult, force = pl.pallas_call(
        functools.partial(kernel, nz, harms),
        out_shape=(
            jax.ShapeDtypeStruct((NB, BLK, COLS), f32),
            jax.ShapeDtypeStruct((CB, BLK, COLS), f32),
        ),
        in_specs=[hbm] * 6,
        out_specs=(OUT, OUT),
        scratch_shapes=scratch,
        compiler_params=pltpu.CompilerParams(
            collective_id=0, has_side_effects=True, vmem_limit_bytes=48 << 20
        ),
    )(
        *(
            pltpu.with_memory_space_constraint(x, pltpu.HBM)
            for x in (
                side,
                partner,
                contact_blocks,
                contact_stiff,
                flex.reshape(NB, BLK, ROWS),
                loads.reshape(NB, BLK, COLS),
            )
        )
    )
    return mult.reshape(loads.shape), force.reshape(1, 1, CROWS, COLS)


def solution(mesh):
    return jax.shard_map(
        per_device,
        mesh=mesh,
        in_specs=(
            P("sub", "harm", None, None),
            P("sub", "harm", None, None),
            P("sub", None),
            P("sub", None),
            P("sub", None),
            P("sub", None),
        ),
        out_specs=(P("sub", "harm", None, None), P("sub", "harm", None, None)),
        check_vma=False,
    )
```

time: 812 us -> 85.6 us (0.11)
  blocking collectives: 511 us -> 0 us
  starting transfers between devices: 103 us -> 0 us
  Pallas kernels: 0 us -> 83.2 us
  waiting for transfers between devices: 81.4 us -> 0 us
  local copies, waits for them, and re-layouts: 49.5 us -> 1.58 us
  other arithmetic: 34.6 us -> 0 us
  matrix products: 29 us -> 0 us
    psum x4 -> x0, blocking collectives: 445 us -> none  [per_device(): lax.psum((jnp.sum(jump * jump, axis=1), jnp.sum(jump * flex_image, axis=1...]
    pallas_call x0 -> x1, Pallas kernels: none -> 83.2 us  [per_device(): pl.pallas_call(functools.partial(kernel, nz, harms), out_shape=(jax.Shape...]
    all_to_all x3 -> x0, starting transfers between devices: 70.4 us -> none  [the longest x1 61.7 us: contact_cycle(): lax.all_to_all(contact_coef, 'harm', split_axis=2, concat_axis=0, tiled=T...]
    ppermute x8 -> x0, waiting for transfers between devices: 66.7 us -> none  [the longest x4 40.7 us: extended(): lax.ppermute(head, axis, [((i + 1) % count, i) for i in range(count)])]
    all_to_all x1 -> x0, blocking collectives: 66.3 us -> none  [contact_cycle(): lax.all_to_all(contact_coef, 'harm', split_axis=2, concat_axis=0, tiled=T...]
    ppermute x8 -> x0, starting transfers between devices: 33.1 us -> none  [the longest x4 24.7 us: extended(): lax.ppermute(head, axis, [((i + 1) % count, i) for i in range(count)])]
    dot_general x13 -> x0, matrix products: 29 us -> none  [the longest x5 21.6 us: apply_flex(): return jnp.einsum('hij,hjc->hic', flex, field, precision=precise)]
    gather x6 -> x0, local copies, waits for them, and re-layouts: 15 us -> none  [the longest x4 12.8 us: opposite_whole(): picked = jax.vmap(lambda one: one[side + 1, partner], in_axes=1)(padded)]
  transfers between devices with their start and end apart: 11 -> 0, of which waited for: 11 -> 0; matrix products, arithmetic and copies ran while one was open for 1% -> 0% of each run, Pallas kernels for 0% -> 0%
where the time goes in v2:
time: 85.6 us; the launch traced here: 85.5 us
  Pallas kernels  83.2 us (97%)
  local copies, waits for them, and re-layouts  1.58 us (2%)
    pallas_call x1, Pallas kernels, per_device(): pl.pallas_call(functools.partial(kernel, nz, harms), out_shape=(jax.Shape...  83.2 us

profile of v2, /device:TPU:1, one launch (start us, length us, event | category | flops | bytes accessed | tf_op | source)
XLA Modules:
  0.0 85.5 jit_solution(18324927478497415611)
XLA Ops:
  0.6 83.2 %shard_map.77 = (f32[12,64,256]{2,1,0:T(8,128)S(1)}, f32[4,64,256]{2,1,0:T(8,128)S(1)}) custom-call(s32[1,12]{1,0:T(1,128)} %side_h.1, s32[1,12]{1,0:T(1,128)} %partner_h.1, s32[1,4]{1,0:T(1,128)} %cblk_h.1, f32[1,256]{1,0:T(1,128)} %stiff_h.1, f32[12,64,768]{2,1,0:T(8,128)} %bitcast.6, f32[12,64,256]{2,1,0:T(8,128)} %bitcast.7), custom_call_target="tpu_custom_call" | custom-call | tf_op jit(solution)/shard_map/pallas_call | solution.py:504
  83.9 0.9 %copy.10 = f32[1,1,768,256]{3,2,1,0:T(8,128)} copy(f32[1,1,768,256]{3,2,1,0:T(8,128)S(1)} %bitcast.4) | data formatting | bytes 1572864
  84.8 0.7 copy.11

commit v3 on v2

--- a/solution.py
+++ b/solution.py
@@ -87,10 +87,12 @@
     side, partner, cblk, tab = take(4)
     stiff, flex, loads, fh, fl, x2, stc, waves = take(8)
     js, ds, gs, tn, ms = (take(NCH) for _ in range(5))
-    imc, gc, tc, old, mo = (take(NCH) for _ in range(5))
+    steps, old, mo = (take(NCH) for _ in range(3))
     snd = [take(NCH) for _ in range(2 * ROUNDS)]
     rcv = [take(NCH) for _ in range(2 * ROUNDS)]
-    sum_y, sum_z, ct, rc, oc, bc = ([take(NCH) for _ in range(ROUNDS)] for _ in range(6))
+    sum_z, sum_y, oc, bc = ([take(NCH) for _ in range(ROUNDS)] for _ in range(4))
+    mine = [[take(3) for _ in range(NCH)] for _ in range(ROUNDS)]
+    all_of = [[take(3) for _ in range(NCH)] for _ in range(ROUNDS)]
     in_sem, ex_s, ex_r, y_s, y_r, z_s, z_r, a_s, a_r = take(9)
     told = take(len(relay_steps(nz)))
 
@@ -103,6 +105,11 @@
     right = (lax.rem(sub + 1, subs), harm)
     left = (lax.rem(sub + subs - 1, subs), harm)
     y_peers = [(my_z * NY + lax.rem(my_y + d, NY), harm) for d in range(1, NY)]
+    pairs = [(d, h) for d in range(NY) for h in range(harms) if d + h > 0]
+    pairs.sort(key=lambda p: -min(p[0], NY - p[0]) - min(p[1], harms - p[1]) / 2)
+    plane_peers = [
+        (my_z * NY + lax.rem(my_y + d, NY), lax.rem(harm + h, harms)) for d, h in pairs
+    ]
     z_order = sorted(range(1, nz), key=lambda d: -min(d, nz - d))
     z_peers = {d: (lax.rem(my_z + d, nz) * NY + my_y, harm) for d in z_order}
     h_order = sorted(range(1, harms), key=lambda d: -min(d, harms - d))
@@ -214,9 +221,28 @@
         tab[4, b] = place
         tab[5, b] = found
 
+    def rows_of(index):
+        return pl.ds(pl.multiple_of(index * part, part), part)
+
+    def to_harm(r, c, i, d):
+        return pltpu.make_async_remote_copy(
+            src_ref=mine[r][c][i].at[rows_of(h_peers[d])],
+            dst_ref=all_of[r][c][i].at[harm],
+            send_sem=a_s.at[r, c, i],
+            recv_sem=a_r.at[r, c, i],
+            device_id=(sub, h_peers[d]),
+            device_id_type=MESH,
+        )
+
+    def share(r, c, i):
+        for d in h_order:
+            to_harm(r, c, i, d).start()
+        all_of[r][c][i][harm] = mine[r][c][i][rows_of(harm), :]
+
     for c in range(NCH):
         for q in range(CB):
-            tc[c][q] = loads[cblk[0, q], :, lanes[c]]
+            mine[0][c][0][pl.ds(q * BLK, BLK), :] = loads[cblk[0, q], :, lanes[c]]
+        share(0, c, 0)
 
     drain(flex, in_sem.at[5])
     lane = lax.broadcasted_iota(jnp.int32, (BLK, 128), 1)
@@ -275,24 +301,37 @@
         acc = jnp.zeros((8, WIDTH), f32)
         return total(lax.fori_loop(0, 2 * MAXB, lambda k, a: a + fold(one[k] * two[k]), acc))
 
-    def product(rows, cols, target, base=None):
+    def product(rows, cols, put_tile):
         x = x2[0 : cols[1] - cols[0], :]
         for at in range(rows[0], rows[1], TILE):
             first = fh[at : at + TILE, cols[0] : cols[1]]
             second = fl[at : at + TILE, cols[0] : cols[1]]
             out = dot(first, x) + dot(second, x)
-            out = (out[:, :WIDTH] + out[:, WIDTH:]).reshape(TILE // BLK, BLK, WIDTH)
-            blocks = pl.ds((at - rows[0]) // BLK, TILE // BLK)
+            put_tile(at - rows[0], out[:, :WIDTH] + out[:, WIDTH:])
+
+    def into_slots(target, base=None):
+        def put_tile(at, out):
+            blocks = pl.ds(at // BLK, TILE // BLK)
+            out = out.reshape(TILE // BLK, BLK, WIDTH)
             target[blocks] = out if base is None else base[blocks] - out
 
-    def y_copy(r, c, d):
-        ref = sum_y[r][c].at[my_y]
+        return put_tile
+
+    def into_rows(target, base=None):
+        def put_tile(at, out):
+            rows = pl.ds(at, TILE)
+            target[rows, :] = out if base is None else base[rows, :] - out
+
+        return put_tile
+
+    def y_copy(r, c, peer):
+        ref = sum_y[r][c].at[my_y * harms + harm]
         return pltpu.make_async_remote_copy(
             src_ref=ref,
             dst_ref=ref,
             send_sem=y_s.at[r, c],
             recv_sem=y_r.at[r, c],
-            device_id=y_peers[d - 1],
+            device_id=peer,
             device_id_type=MESH,
         )
 
@@ -307,25 +346,12 @@
             device_id_type=MESH,
         )
 
-    def rows_of(index):
-        return pl.ds(pl.multiple_of(index * part, part), part)
-
-    def to_harm(r, c, d):
-        return pltpu.make_async_remote_copy(
-            src_ref=ct[r][c].at[rows_of(h_peers[d])],
-            dst_ref=rc[r][c].at[harm],
-            send_sem=a_s.at[r, c, 0],
-            recv_sem=a_r.at[r, c, 0],
-            device_id=(sub, h_peers[d]),
-            device_id_type=MESH,
-        )
-
     def from_harm(r, c, d):
         return pltpu.make_async_remote_copy(
             src_ref=oc[r][c].at[h_peers[d]],
             dst_ref=bc[r][c].at[rows_of(harm)],
-            send_sem=a_s.at[r, c, 1],
-            recv_sem=a_r.at[r, c, 1],
+            send_sem=a_s.at[r, c, 3],
+            recv_sem=a_r.at[r, c, 3],
             device_id=(sub, h_peers[d]),
             device_id_type=MESH,
         )
@@ -336,7 +362,12 @@
         @pl.loop(0, part // 16)
         def _(i):
             rows = pl.ds(pl.multiple_of(i * 16, 16), 16)
-            coefs = [rc[r][c][k, rows, :].reshape(2, 8, 128) for k in range(harms)]
+            coefs = []
+            for k in range(harms):
+                trace, image, second = (
+                    all_of[r][c][n][k, rows, :].reshape(2, 8, 128) for n in range(3)
+                )
+                coefs.append(trace - steps[c][0, k] * image + steps[c][1, k] * second)
             for k, value in enumerate(cube_law(coefs, waves, odd)):
                 oc[r][c][k, rows, :] = value.reshape(16, 128)
 
@@ -345,16 +376,17 @@
     def stage_jump(r, c):
         drain(rcv[2 * r][c], ex_r.at[2 * r, c])
         square = difference(2 * r, c, js[c])
-        product(shared, shared, snd[2 * r + 1][c])
+        product(shared, shared, into_slots(snd[2 * r + 1][c]))
         send(2 * r + 1, c)
-        product(joint, shared, imc[c])
+        product(joint, shared, into_rows(mine[r][c][1]))
+        share(r, c, 1)
         sum_z[r][c][my_z, 0:1, :] = square
         sum_z[r][c][my_z, 1:2, :] = inner(js[c], snd[2 * r + 1][c])
 
     def stage_image(r, c):
         drain(rcv[2 * r + 1][c], ex_r.at[2 * r + 1, c])
         square = difference(2 * r + 1, c, ds[c])
-        product(shared, shared, gs[c])
+        product(shared, shared, into_slots(gs[c]))
         sum_z[r][c][my_z, 2:3, :] = square
         sum_z[r][c][my_z, 3:4, :] = inner(ds[c], gs[c])
         if r == 0 and c == 0:
@@ -362,29 +394,37 @@
             assert len(told) <= 2
         for d in z_order:
             z_copy(r, c, d).start()
-        product(joint, shared, gc[c])
+        product(joint, shared, into_rows(mine[r][c][2]))
+        share(r, c, 2)
 
     def stage_sums(r, c):
+        for i in range(2):
+            drain(all_of[r][c][i].at[pl.ds(0, harms - 1)], a_r.at[r, c, i])
         drain(sum_z[r][c].at[pl.ds(0, nz - 1)], z_r.at[r, c])
-        sum_y[r][c][my_y] = jnp.sum(sum_z[r][c][...], axis=0)
-        for d in range(1, NY):
-            y_copy(r, c, d).start()
-
-    def stage_step(r, c):
-        drain(sum_y[r][c].at[pl.ds(0, NY - 1)], y_r.at[r, c])
-        value = jnp.sum(sum_y[r][c][...], axis=0)
-        square, curve, square_d, curve_d = (value[i : i + 1] for i in range(4))
+        sum_y[r][c][my_y * harms + harm] = jnp.sum(sum_z[r][c][...], axis=0)
+        for peer in plane_peers:
+            y_copy(r, c, peer).start()
+
+    def stage_contact(r, c):
+        drain(sum_y[r][c].at[pl.ds(0, NY * harms - 1)], y_r.at[r, c])
+        value = sum_y[r][c][0:harms]
+        for y in range(1, NY):
+            value = value + sum_y[r][c][y * harms : (y + 1) * harms]
+        square, curve, square_d, curve_d = (value[:, i : i + 1] for i in range(4))
         first = square / (curve + TINY)
         square = square - 4.0 * first * curve + first * first * square_d
         curve = curve - first * square_d + first * first * curve_d
         second = square / (curve + TINY)
-        both, cross = first + second, first * second
-        for q in range(CB):
-            value = tc[c][q] - both * imc[c][q] + cross * gc[c][q]
-            ct[r][c][pl.ds(q * BLK, BLK), :] = value
+        steps[c][0] = jnp.broadcast_to(first + second, (harms, 8, WIDTH))
+        steps[c][1] = jnp.broadcast_to(first * second, (harms, 8, WIDTH))
+        drain(all_of[r][c][2].at[pl.ds(0, harms - 1)], a_r.at[r, c, 2])
+        contact(r, c)
         for d in h_order:
-            to_harm(r, c, d).start()
-        rc[r][c][harm] = ct[r][c][rows_of(harm), :]
+            from_harm(r, c, d).start()
+        bc[r][c][rows_of(harm), :] = oc[r][c][harm]
+
+    def stage_step(r, c):
+        both, cross = steps[c][0, harm][0:1], steps[c][1, harm][0:1]
 
         @pl.loop(0, 2 * MAXB)
         def _(k):
@@ -394,37 +434,32 @@
                 image = snd[2 * r + 1][c][k]
                 tn[c][k] = snd[2 * r][c][k] - both * image + cross * gs[c][k]
 
-        if r + 1 == ROUNDS:
+        if r + 1 < ROUNDS:
+            trace, image, second = (mine[r][c][n][...] for n in range(3))
+            mine[r + 1][c][0][...] = trace - both * image + cross * second
+        else:
 
             @pl.loop(0, NB)
             def _(b):
                 value = jnp.where(tab[3, b] != 0, ms[c][tab[2, b]], 0.0)
                 mo[c][b] = value - jnp.where(tab[5, b] != 0, old[c][tab[4, b]], 0.0)
 
-    def stage_contact(r, c):
-        drain(rc[r][c].at[pl.ds(0, harms - 1)], a_r.at[r, c, 0])
-        contact(r, c)
-        for d in h_order:
-            from_harm(r, c, d).start()
-        bc[r][c][rows_of(harm), :] = oc[r][c][harm]
-
     def stage_force(r, c):
-        drain(bc[r][c].at[pl.ds(0, (harms - 1) * part)], a_r.at[r, c, 1])
+        drain(bc[r][c].at[pl.ds(0, (harms - 1) * part)], a_r.at[r, c, 3])
         for q in range(CB):
             rows = pl.ds(q * BLK, BLK)
             value = bc[r][c][rows, :] * stc[rows, :]
+            old[c][q] = value
             if r + 1 < ROUNDS:
-                old[c][q] = value
                 put(q, value)
             else:
-                old[c][q] = value
                 force[q, :, lanes[c]] = value
         if r + 1 < ROUNDS:
-            product(shared, joint, snd[2 * r + 2][c], tn[c])
+            product(shared, joint, into_slots(snd[2 * r + 2][c], tn[c]))
             send(2 * r + 2, c)
-            for q in range(CB):
-                tc[c][q] = ct[r][c][pl.ds(q * BLK, BLK), :]
-            product(joint, joint, tc[c], tc[c])
+            rows = mine[r + 1][c][0]
+            product(joint, joint, into_rows(rows, rows))
+            share(r + 1, c, 0)
         else:
 
             @pl.loop(0, NB)
@@ -436,12 +471,13 @@
         if r > 0 or c > 0:
             drain(snd[2 * r][c], ex_s.at[2 * r, c])
         drain(snd[2 * r + 1][c], ex_s.at[2 * r + 1, c])
-        drain(sum_y[r][c].at[pl.ds(0, NY - 1)], y_s.at[r, c])
+        drain(sum_y[r][c].at[pl.ds(0, NY * harms - 1)], y_s.at[r, c])
         drain(sum_z[r][c].at[pl.ds(0, nz - 1)], z_s.at[r, c])
-        drain(ct[r][c].at[pl.ds(0, (harms - 1) * part)], a_s.at[r, c, 0])
+        for i in range(3):
+            drain(mine[r][c][i].at[pl.ds(0, (harms - 1) * part)], a_s.at[r, c, i])
 
     def settle_last(r, c):
-        drain(oc[r][c].at[pl.ds(0, harms - 1)], a_s.at[r, c, 1])
+        drain(oc[r][c].at[pl.ds(0, harms - 1)], a_s.at[r, c, 3])
 
     for r in range(ROUNDS):
         for c in every:
@@ -454,11 +490,9 @@
             stage_image(r, c)
         for c in every:
             stage_sums(r, c)
-            if c > 0:
-                stage_step(r, c - 1)
-        stage_step(r, NCH - 1)
         for c in every:
             stage_contact(r, c)
+            stage_step(r, c)
         if r == ROUNDS - 1:
             for c in every:
                 settle(r, c)
@@ -491,14 +525,15 @@
         pltpu.VMEM((CROWS, WIDTH), f32),
         pltpu.VMEM((TIMES // 4 + 1, harms, 8, 128), f32),
     ]
-    scratch += slots * 5 + joint * 4 + whole
+    scratch += slots * 5 + [pltpu.VMEM((2, harms, 8, WIDTH), f32)] * NCH + joint + whole
     scratch += slots * (2 * ROUNDS) * 2
-    scratch += vmem(NY, 4, WIDTH) + vmem(nz, 4, WIDTH)
-    scratch += vmem(CROWS, WIDTH) + vmem(harms, part, WIDTH) * 2 + vmem(CROWS, WIDTH)
+    scratch += vmem(nz, 4, WIDTH) + vmem(NY * harms, 4, WIDTH)
+    scratch += vmem(harms, part, WIDTH) + vmem(CROWS, WIDTH)
+    scratch += vmem(CROWS, WIDTH) * 3 + vmem(harms, part, WIDTH) * 3
     scratch += [sem((6,))]
     scratch += [sem((2 * ROUNDS, NCH))] * 2
     scratch += [sem((ROUNDS, NCH))] * 4
-    scratch += [sem((ROUNDS, NCH, 2))] * 2
+    scratch += [sem((ROUNDS, NCH, 4))] * 2
     scratch += [pltpu.SemaphoreType.REGULAR] * len(relay_steps(nz))
     hbm = pl.BlockSpec(memory_space=pltpu.HBM)
     mult, force = pl.pallas_call(

time: 85.6 us -> 80.4 us (0.939)
  Pallas kernels: 83.2 us -> 78 us
    pallas_call x1, Pallas kernels: 83.2 us -> 78 us  [per_device(): pl.pallas_call(functools.partial(kernel, nz, harms), out_shape=(jax.Shape...]
where the time goes in v3:
time: 80.4 us; the launch traced here: 80.3 us
  Pallas kernels  78 us (97%)
  local copies, waits for them, and re-layouts  1.58 us (2%)
    pallas_call x1, Pallas kernels, per_device(): pl.pallas_call(functools.partial(kernel, nz, harms), out_shape=(jax.Shape...  78 us

profile of v3, /device:TPU:1, one launch (start us, length us, event | category | flops | bytes accessed | tf_op | source)
XLA Modules:
  0.0 80.3 jit_solution(15749958859613507466)
XLA Ops:
  0.6 78.0 %shard_map.77 = (f32[12,64,256]{2,1,0:T(8,128)S(1)}, f32[4,64,256]{2,1,0:T(8,128)S(1)}) custom-call(s32[1,12]{1,0:T(1,128)} %side_h.1, s32[1,12]{1,0:T(1,128)} %partner_h.1, s32[1,4]{1,0:T(1,128)} %cblk_h.1, f32[1,256]{1,0:T(1,128)} %stiff_h.1, f32[12,64,768]{2,1,0:T(8,128)} %bitcast.6, f32[12,64,256]{2,1,0:T(8,128)} %bitcast.7), custom_call_target="tpu_custom_call" | custom-call | tf_op jit(solution)/shard_map/pallas_call | solution.py:539
  78.7 0.9 %copy.10 = f32[1,1,768,256]{3,2,1,0:T(8,128)} copy(f32[1,1,768,256]{3,2,1,0:T(8,128)S(1)} %bitcast.4) | data formatting | bytes 1572864
  79.6 0.7 copy.11

commit v4 on v3

--- a/solution.py
+++ b/solution.py
@@ -23,7 +23,7 @@
 NCH = 2
 WIDTH = COLS // NCH
 S_ROWS = 2 * MAXB * BLK
-TILE = 256
+TILE = 128
 PAIRS = ROWS // 128
 OUT = pl.BlockSpec(memory_space=pltpu.VMEM)
 
@@ -133,15 +133,13 @@
         )
         for i in range(PAIRS)
     ]
-    for copy in copies[:3]:
-        copy.start()
     barrier = pltpu.get_barrier_semaphore()
     near = [d for d in z_order if min(d, nz - d) <= 2]
     greet = [right, left] + [z_peers[d] for d in near] + y_peers + [(sub, h_peers[d]) for d in h_order]
     for peer in greet:
         signal(barrier, peer)
 
-    for copy in copies[3:]:
+    for copy in copies:
         copy.start()
     for copy in copies[:3]:
         copy.wait()
@@ -500,6 +498,17 @@
             stage_force(r, c)
     for c in every:
         settle_last(ROUNDS - 1, c)
+
+
+def write_out(mult_v, force_v, mult, force, sem):
+    copies = [
+        pltpu.make_async_copy(mult_v, mult, sem.at[0]),
+        pltpu.make_async_copy(force_v, force, sem.at[1]),
+    ]
+    for copy in copies:
+        copy.start()
+    for copy in copies:
+        copy.wait()
 
 
 def per_device(flex, loads, side, partner, contact_blocks, contact_stiff):
@@ -561,6 +570,17 @@
             )
         )
     )
+    mult, force = pl.pallas_call(
+        write_out,
+        out_shape=(
+            jax.ShapeDtypeStruct((NB, BLK, COLS), f32),
+            jax.ShapeDtypeStruct((CB, BLK, COLS), f32),
+        ),
+        in_specs=[pl.BlockSpec(memory_space=pl.ANY)] * 2,
+        out_specs=[pl.BlockSpec(memory_space=pl.ANY)] * 2,
+        scratch_shapes=[pltpu.SemaphoreType.DMA((2,))],
+        compiler_params=pltpu.CompilerParams(vmem_limit_bytes=1 << 20),
+    )(mult, force)
     return mult.reshape(loads.shape), force.reshape(1, 1, CROWS, COLS)
 
 

time: 80.4 us -> 80 us (level)
  local copies, waits for them, and re-layouts: 1.58 us -> 0 us
  Pallas kernels: 78 us -> 79.2 us
    unnamed x2 -> x0, local copies, waits for them, and re-layouts: 1.58 us -> none
    pallas_call x0 -> x1, Pallas kernels: none -> 0.98 us  [per_device(): pl.pallas_call(write_out, out_shape=(jax.ShapeDtypeStruct((NB, BLK, COLS)...]
where the time goes in v4:
time: 80 us; the launch traced here: 79.8 us
  Pallas kernels  79.2 us (99%)
    pallas_call x1, Pallas kernels, per_device(): pl.pallas_call(functools.partial(kernel, nz, harms), out_shape=(jax.Shape...  78.2 us

profile of v4, /device:TPU:1, one launch (start us, length us, event | category | flops | bytes accessed | tf_op | source)
XLA Modules:
  0.0 79.8 jit_solution(5005524320269772333)
XLA Ops:
  0.6 78.2 %shard_map.77 = (f32[12,64,256]{2,1,0:T(8,128)S(1)}, f32[4,64,256]{2,1,0:T(8,128)S(1)}) custom-call(s32[1,12]{1,0:T(1,128)} %side_h.1, s32[1,12]{1,0:T(1,128)} %partner_h.1, s32[1,4]{1,0:T(1,128)} %cblk_h.1, f32[1,256]{1,0:T(1,128)} %stiff_h.1, f32[12,64,768]{2,1,0:T(8,128)} %bitcast.4, f32[12,64,256]{2,1,0:T(8,128)} %bitcast.5), custom_call_target="tpu_custom_call" | custom-call | tf_op jit(solution)/shard_map/pallas_call | solution.py:548
  78.9 1.0 %shard_map.78 = (f32[12,64,256]{2,1,0:T(8,128)}, f32[4,64,256]{2,1,0:T(8,128)}) custom-call(f32[12,64,256]{2,1,0:T(8,128)S(1)} %get-tuple-element.6.mult_v, f32[4,64,256]{2,1,0:T(8,128)S(1)} %get-tuple-element.7.force_v), custom_call_target="tpu_custom_call" | custom-call | tf_op jit(solution)/shard_map/pallas_call | solution.py:573

commit v5 on v4

--- a/solution.py
+++ b/solution.py
@@ -172,10 +172,10 @@
         tab[1, k] = jnp.where(k % MAXB < (count_r if k < MAXB else count_l), one, zero)
     for q in range(CB):
         tab[0, 2 * MAXB + q] = contacts[q]
-    def exchange(e, c, way):
+    def exchange(e, c, way, half):
         return pltpu.make_async_remote_copy(
-            src_ref=snd[e][c].at[pl.ds(way * MAXB, MAXB)],
-            dst_ref=rcv[e][c].at[pl.ds((1 - way) * MAXB, MAXB)],
+            src_ref=snd[e][c].at[pl.ds(way * MAXB + 2 * half, 2)],
+            dst_ref=rcv[e][c].at[pl.ds((1 - way) * MAXB + 2 * half, 2)],
             send_sem=ex_s.at[e, c],
             recv_sem=ex_r.at[e, c],
             device_id=right if way == 0 else left,
@@ -194,8 +194,9 @@
             tell(i + 1)
 
     def send(e, c):
-        for way in range(2):
-            exchange(e, c, way).start()
+        for half in range(2):
+            for way in range(2):
+                exchange(e, c, way, half).start()
 
     copies[3].wait()
     lanes = [pl.ds(c * WIDTH, WIDTH) for c in range(NCH)]
@@ -301,17 +302,21 @@
 
     def product(rows, cols, put_tile):
         x = x2[0 : cols[1] - cols[0], :]
-        for at in range(rows[0], rows[1], TILE):
+        tiles = list(range(rows[0], rows[1], TILE))
+        for at in tiles[0::2] + tiles[1::2]:
             first = fh[at : at + TILE, cols[0] : cols[1]]
             second = fl[at : at + TILE, cols[0] : cols[1]]
             out = dot(first, x) + dot(second, x)
             put_tile(at - rows[0], out[:, :WIDTH] + out[:, WIDTH:])
 
-    def into_slots(target, base=None):
+    def into_slots(target, base=None, sent=None):
         def put_tile(at, out):
             blocks = pl.ds(at // BLK, TILE // BLK)
             out = out.reshape(TILE // BLK, BLK, WIDTH)
             target[blocks] = out if base is None else base[blocks] - out
+            if sent is not None:
+                first = at // BLK
+                exchange(*sent, first // MAXB, first % MAXB // 2).start()
 
         return put_tile
 
@@ -374,8 +379,7 @@
     def stage_jump(r, c):
         drain(rcv[2 * r][c], ex_r.at[2 * r, c])
         square = difference(2 * r, c, js[c])
-        product(shared, shared, into_slots(snd[2 * r + 1][c]))
-        send(2 * r + 1, c)
+        product(shared, shared, into_slots(snd[2 * r + 1][c], sent=(2 * r + 1, c)))
         product(joint, shared, into_rows(mine[r][c][1]))
         share(r, c, 1)
         sum_z[r][c][my_z, 0:1, :] = square
@@ -453,8 +457,7 @@
             else:
                 force[q, :, lanes[c]] = value
         if r + 1 < ROUNDS:
-            product(shared, joint, into_slots(snd[2 * r + 2][c], tn[c]))
-            send(2 * r + 2, c)
+            product(shared, joint, into_slots(snd[2 * r + 2][c], tn[c], (2 * r + 2, c)))
             rows = mine[r + 1][c][0]
             product(joint, joint, into_rows(rows, rows))
             share(r + 1, c, 0)

time: 80 us -> 79.9 us (level)
  no operation moved by 1% of the time
where the time goes in v5:
time: 79.9 us; the launch traced here: 79.8 us
  Pallas kernels  79.1 us (99%)
    pallas_call x1, Pallas kernels, per_device(): pl.pallas_call(functools.partial(kernel, nz, harms), out_shape=(jax.Shape...  78.1 us

profile of v5, /device:TPU:1, one launch (start us, length us, event | category | flops | bytes accessed | tf_op | source)
XLA Modules:
  0.0 79.8 jit_solution(10203162643630853424)
XLA Ops:
  0.6 78.1 %shard_map.77 = (f32[12,64,256]{2,1,0:T(8,128)S(1)}, f32[4,64,256]{2,1,0:T(8,128)S(1)}) custom-call(s32[1,12]{1,0:T(1,128)} %side_h.1, s32[1,12]{1,0:T(1,128)} %partner_h.1, s32[1,4]{1,0:T(1,128)} %cblk_h.1, f32[1,256]{1,0:T(1,128)} %stiff_h.1, f32[12,64,768]{2,1,0:T(8,128)} %bitcast.4, f32[12,64,256]{2,1,0:T(8,128)} %bitcast.5), custom_call_target="tpu_custom_call" | custom-call | tf_op jit(solution)/shard_map/pallas_call | solution.py:551
  78.8 1.0 %shard_map.78 = (f32[12,64,256]{2,1,0:T(8,128)}, f32[4,64,256]{2,1,0:T(8,128)}) custom-call(f32[12,64,256]{2,1,0:T(8,128)S(1)} %get-tuple-element.6.mult_v, f32[4,64,256]{2,1,0:T(8,128)S(1)} %get-tuple-element.7.force_v), custom_call_target="tpu_custom_call" | custom-call | tf_op jit(solution)/shard_map/pallas_call | solution.py:576
